TPU v7x, 32 devices: a whole 2x2x4 slice. The times are simulated.
32 devices in a mesh: region: 4 (over y, x), cluster: 8 (over z, core).
Axes of the slice: x: 2, y: 2, z: 4, core: 2. Of those that a mesh axis runs over, the one named last changes fastest.
Arguments:
- pilots: bfloat16 [128, 1024, 1024], P(('region', 'cluster')), may hold values from -0.1875 to 0.1875
- estimate: bfloat16 [128, 8, 1024], P(('region', 'cluster')), may hold values from -6 to 6
- visible: int32 [128, 1024], P(('region', 'cluster')), may hold values from 0 to 65535, as said below
- blocks: int32 [128], P(('region', 'cluster')), may hold values from 4 to 8
- received: float32 [128, 8, 1024], P(('region', 'cluster')), may hold values from -6 to 6
- previous: float32 [128, 8, 1024], P(('region', 'cluster')), may hold values from -6 to 6
- onsager: float32 [128], P(('region', 'cluster')), may hold values from 0.2 to 0.8
- user_cluster: int32 [65536], replicated, may hold values from 0 to 15
- cluster_prior: float32 [16], replicated, may hold values from -4 to 0
Outputs:
- new_estimate: bfloat16 [128, 8, 1024], P(('region', 'cluster'))
- residual: float32 [128, 8, 1024], P(('region', 'cluster'))
- posterior: float32 [65536], P(('region', 'cluster'))
Inputs may be any that keep to these rules, and one draw needn't show every extreme that they name: Every draw has some access point with 8 live blocks. `visible`: users are numbered region by region, 2048 * 8 to a region, in the order of the devices along region+cluster. An access point hears only users of its own region or of the two regions beside it along region (the first and the last region are beside each other); most of the users it hears are of its own region.
All inputs are finite; a program needn't handle non-finite values.
Results may differ from a plain program's by a relative error of at most 0.0056.
Values sent between devices are 32-bit elements; how exact they have to be, the bound alone decides.
A program may use at most 192 MiB of HBM per device.

v0:
```python
import jax
import jax.numpy as jnp
from jax import lax
from jax.sharding import PartitionSpec as P

ROW_BLOCK = 128
U_DEV = 2048
epsilon = 1e-06


def passed_along(block, axis, distance):
    devices = range(lax.axis_size(axis))
    route = [((i - distance) % len(devices), i) for i in devices]
    return lax.ppermute(block, axis, route)


def decide(summed, start, count, user_cluster, cluster_prior):
    labels = lax.dynamic_slice_in_dim(user_cluster, start, count)
    table = jnp.arange(cluster_prior.shape[0], dtype=jnp.int32)
    prior = jnp.sum(
        jnp.where(labels[:, None] == table[None, :], cluster_prior[None, :], jnp.float32(0.0)),
        axis=1,
    )
    return jax.nn.sigmoid(summed + prior)


def local(
    pilots, estimate, visible, blocks, received, previous, onsager, user_cluster, cluster_prior
):
    points, antennas, slots = estimate.shape
    live = jnp.arange(slots)[None, :] // ROW_BLOCK < blocks[:, None]
    masked = jnp.where(live[:, None, :], estimate, jnp.zeros_like(estimate))
    widened = masked.astype(jnp.float32)
    product = jnp.einsum("amr,arl->aml", masked, pilots, preferred_element_type=jnp.float32)
    resid = received - product + onsager[:, None, None] * previous
    spread = jnp.mean(resid * resid, axis=(1, 2)) + epsilon
    narrow = resid.astype(jnp.bfloat16)
    stat = widened + jnp.einsum("aml,arl->amr", narrow, pilots, preferred_element_type=jnp.float32)
    energy = jnp.sum(stat * stat, axis=1)
    base = 0.5 * antennas * jnp.log(spread / (1.0 + spread))
    llr = base[:, None] + energy / (2.0 * spread * (1.0 + spread))[:, None]
    llr = jnp.where(live, llr, jnp.float32(0.0))
    total_users = U_DEV * lax.axis_size("region") * lax.axis_size("cluster")
    own_start = lax.axis_index(("region", "cluster")) * U_DEV
    flat_llr = llr.reshape(-1)
    region_users = U_DEV * lax.axis_size("cluster")
    regions = lax.axis_size("region")
    lowest = (lax.axis_index("region") + regions - 1) % regions * region_users
    relative = (visible - lowest + total_users) % total_users
    window = jax.ops.segment_sum(flat_llr, relative.reshape(-1), num_segments=3 * region_users)
    from_below = passed_along(window[2 * region_users :], "region", 1)
    from_above = passed_along(window[:region_users], "region", -1)
    region_sum = window[region_users : 2 * region_users] + from_below + from_above
    owned_sum = lax.psum_scatter(region_sum, "cluster", scatter_dimension=0, tiled=True)
    owned = decide(owned_sum, own_start, U_DEV, user_cluster, cluster_prior)
    own_post = lax.all_gather(owned, "cluster", axis=0, tiled=True)
    below = passed_along(own_post, "region", 1)
    above = passed_along(own_post, "region", -1)
    nearby = jnp.concatenate([below, own_post, above])
    rate = nearby[relative]
    fresh = rate[:, None, :] * stat / (1.0 + spread)[:, None, None]
    new_estimate = jnp.where(live[:, None, :], fresh, jnp.float32(0.0)).astype(jnp.bfloat16)
    return (new_estimate, resid, owned)


def solution(mesh):
    placed = (
        P(("region", "cluster"), None, None),
        P(("region", "cluster"), None, None),
        P(("region", "cluster"), None),
        P(("region", "cluster")),
        P(("region", "cluster"), None, None),
        P(("region", "cluster"), None, None),
        P(("region", "cluster")),
        P(),
        P(),
    )
    return jax.shard_map(
        local,
        mesh=mesh,
        in_specs=placed,
        out_specs=(
            P(("region", "cluster"), None, None),
            P(("region", "cluster"), None, None),
            P(("region", "cluster")),
        ),
        check_vma=False,
    )
```

profile of v0, /device:TPU:0, one launch (start us, length us, event | category | flops | bytes accessed | tf_op | source)
XLA Modules:
  0.0 153.7 jit_solution(528623752502533669)
XLA Ops:
  7.2 0.0 copy-start.2
  7.2 0.0 all-reduce.3.cloned.1.call-start
  7.3 0.0 copy-start
  7.3 0.9 fusion.7
  8.2 0.9 broadcast_compare_fusion
  9.1 0.0 copy-start.4
  9.1 0.0 copy-start.5
  9.1 0.0 copy-start.6
  9.1 5.3 %multiply_reduce_fusion.1 = (f32[4]{0:T(128)S(1)}, f32[4,8,1024]{2,1,0:T(8,128)S(1)}) fusion(f32[4,8,1024]{2,1,0:T(8,128)} %param.14, f32[4]{0:T(128)} %param.15, f32[4,8,1024]{2,1,0:T(8,128)} %param.13, bf16[4,1024,1024]{2,1,0:T(8,128)(2,1)} %param.9, bf16[4,8,1024]{2,1,0:T(8,128)(2,1)} %param.10, pred[4,1024]{1,0:T(4,128)(4,1)S(1)} %broadcast_compare_fusion), kind=kOutput, calls=%fused_computation.10 | convolution fusion | flops 67305472 | bytes 8851488 | tf_op jit(solution)/shard_map/amr,arl->aml/dot_general | solution.py:34
  14.4 0.0 copy-start.1
  14.4 0.0 copy-done.2
  14.4 0.0 copy-done
  14.4 2.3 %multiply_reduce_fusion = (f32[4,1024]{1,0:T(4,128)S(1)}, f32[4,8,1024]{2,1,0:T(8,128)S(1)}) fusion(bf16[4,1024,1024]{2,1,0:T(8,128)(2,1)S(1)} %copy-done, f32[4,8,1024]{2,1,0:T(8,128)S(1)} %get-tuple-element.11, bf16[4,8,1024]{2,1,0:T(8,128)(2,1)S(1)} %copy-done.2, pred[4,1024]{1,0:T(4,128)(4,1)S(1)} %broadcast_compare_fusion), kind=kOutput, calls=%fused_computation.9 | convolution fusion | flops 67301376 | bytes 8736768 | tf_op jit(solution)/shard_map/aml,arl->amr/dot_general | solution.py:38
  16.7 0.0 copy-done.4
  16.7 0.1 select_bitcast_fusion
  16.8 21.9 %scatter_custom_fusion = f32[49152]{0:T(1024)S(1)} fusion(s32[4096]{0:T(1024)S(1)} %bitcast.17, f32[4096]{0:T(1024)S(1)} %bitcast.18, f32[]{:T(128)} %constant.68.clone.1), kind=kCustom, calls=%fused_computation.11 | custom fusion | flops 4096 | bytes 196612 | tf_op jit(solution)/shard_map/scatter-add | solution.py:50
  38.8 3.0 %collective-permute-start = (f32[16384]{0:T(1024)S(1)}, f32[16384]{0:T(1024)S(1)}, u32[]{:S(2)}, u32[]{:S(2)}) collective-permute-start(f32[16384]{0:T(1024)S(1)} %get-tuple-element.3), channel_id=1, source_target_pairs={{24,0},{0,8},{8,16},{16,24},{25,1},{1,9},{9,17},{17,25},{26,2},{2,... | collective-permute-start | bytes 196616 | tf_op jit(solution)/shard_map/ppermute | solution.py:14
  41.8 1.0 collective-permute-start.1
  42.8 0.7 dynamic_slice.3
  43.5 1.6 %collective-permute-done = f32[16384]{0:T(1024)S(1)} collective-permute-done((f32[16384]{0:T(1024)S(1)}, f32[16384]{0:T(1024)S(1)}, u32[]{:S(2)}, u32[]{:S(2)}) %collective-permute-start) | collective-permute-done | bytes 65568 | tf_op jit(solution)/shard_map/ppermute | solution.py:14
  45.1 1.4 collective-permute-done.1
  46.5 0.6 fusion.3
  47.1 0.0 all-reduce.3.cloned.1.call-update
  47.2 0.0 copy-done.5
  47.2 0.1 select_reduce_fusion
  47.3 0.0 copy-done.6
  47.3 0.6 dynamic-slice
  48.5 53.2 %all-reduce.3.cloned.1.call-done = f32[16384]{0:T(1024)} async-done(((f32[16384]{0:T(1024)}), f32[16384]{0:T(1024)}) %all-reduce.3.cloned.1.call-update) | async-done | bytes 65552
  101.7 0.7 fusion.11
  102.4 0.0 copy-start.3
  102.4 14.0 %all_gather.3 = f32[16384]{0:T(1024)S(1)} all-gather(f32[2048]{0:T(1024)S(1)} %fusion.11), channel_id=1, replica_groups=mesh['region'=4,'cluster'=8] {'cluster'}, dimensions={0}, use_global_device_ids=true | all-gather | bytes 73728 | tf_op jit(solution)/shard_map/all_gather | solution.py:56
  116.4 1.5 collective-permute-start.2
  117.8 1.5 collective-permute-start.3
  119.3 2.6 %collective-permute-done.2 = f32[16384]{0:T(1024)S(1)} collective-permute-done((f32[16384]{0:T(1024)S(1)}, f32[16384]{0:T(1024)S(1)}, u32[]{:S(2)}, u32[]{:S(2)}) %collective-permute-start.2) | collective-permute-done | bytes 65568 | tf_op jit(solution)/shard_map/ppermute | solution.py:14
  121.9 1.1 collective-permute-done.3
  123.0 23.0 %gather_fusion = f32[4096]{0:T(1024)S(1)} fusion(f32[49152]{0:T(1024)S(1)} %pad_maximum_fusion, s32[4096]{0:T(1024)S(1)} %bitcast_clamp_fusion), kind=kCustom, calls=%fused_computation | custom fusion | bytes 49152 | tf_op jit(solution)/shard_map/gather | solution.py:60
  146.1 0.0 copy-done.1
  146.1 0.0 copy-done.3
  146.1 0.7 select_convert_fusion
  (8 shorter events, 0.1 us)
Async XLA Ops:
  7.2 7.2 %copy-start.2 = (bf16[4,8,1024]{2,1,0:T(8,128)(2,1)S(1)}, bf16[4,8,1024]{2,1,0:T(8,128)(2,1)}, u32[]{:S(2)}) copy-start(bf16[4,8,1024]{2,1,0:T(8,128)(2,1)} %param.10) | copy-start | bytes 196612
  7.2 94.5 %all-reduce.3.cloned.1.call-start = ((), (), s32[]{:S(2)}) async-start(), calls=%async_computation | async-start | bytes 131072
  7.3 7.1 %copy-start = (bf16[4,1024,1024]{2,1,0:T(8,128)(2,1)S(1)}, bf16[4,1024,1024]{2,1,0:T(8,128)(2,1)}, u32[]{:S(2)}) copy-start(bf16[4,1024,1024]{2,1,0:T(8,128)(2,1)} %param.9) | copy-start | bytes 25165828
  9.1 7.7 %copy-start.4 = (s32[4]{0:T(128)S(1)}, s32[4]{0:T(128)}, u32[]{:S(2)}) copy-start(s32[4]{0:T(128)} %param.12) | copy-start | bytes 52
  9.1 38.1 %copy-start.5 = (f32[16]{0:T(128)S(1)}, f32[16]{0:T(128)}, u32[]{:S(2)}) copy-start(f32[16]{0:T(128)} %param.17) | copy-start | bytes 196
  9.1 38.2 %copy-start.6 = (u32[32]{0:T(128)S(1)}, u32[32]{0:T(128)}, u32[]{:S(2)}) copy-start(u32[32]{0:T(128)} %constant.94) | copy-start | bytes 388
  14.4 131.7 %copy-start.1 = (f32[4,8,1024]{2,1,0:T(8,128)}, f32[4,8,1024]{2,1,0:T(8,128)S(1)}, u32[]{:S(2)}) copy-start(f32[4,8,1024]{2,1,0:T(8,128)S(1)} %get-tuple-element.11) | copy-start | bytes 393220
  38.8 6.3 %collective-permute-start = (f32[16384]{0:T(1024)S(1)}, f32[16384]{0:T(1024)S(1)}, u32[]{:S(2)}, u32[]{:S(2)}) collective-permute-start(f32[16384]{0:T(1024)S(1)} %get-tuple-element.3), channel_id=1, source_target_pairs={{24,0},{0,8},{8,16},{16,24},{25,1},{1,9},{9,17},{17,25},{26,2},{2,... | collective-permute-start | bytes 196616 | tf_op jit(solution)/shard_map/ppermute | solution.py:14
  41.8 4.7 %collective-permute-start.1 = (f32[16384]{0:T(1024)S(1)}, f32[16384]{0:T(1024)S(1)}, u32[]{:S(2)}, u32[]{:S(2)}) collective-permute-start(f32[16384]{0:T(1024)S(1)} %get-tuple-element.4), channel_id=1, source_target_pairs={{8,0},{16,8},{24,16},{0,24},{9,1},{17,9},{25,17},{1,25},{10,2},{18... | collective-permute-start | bytes 196616 | tf_op jit(solution)/shard_map/ppermute | solution.py:14
  102.4 43.7 %copy-start.3 = (f32[2048]{0:T(1024)}, f32[2048]{0:T(1024)S(1)}, u32[]{:S(2)}) copy-start(f32[2048]{0:T(1024)S(1)} %fusion.11) | copy-start | bytes 24580
  116.4 5.5 %collective-permute-start.2 = (f32[16384]{0:T(1024)S(1)}, f32[16384]{0:T(1024)S(1)}, u32[]{:S(2)}, u32[]{:S(2)}) collective-permute-start(f32[16384]{0:T(1024)S(1)} %all_gather.3), channel_id=1, source_target_pairs={{24,0},{0,8},{8,16},{16,24},{25,1},{1,9},{9,17},{17,25},{26,2},{2,... | collective-permute-start | bytes 196616 | tf_op jit(solution)/shard_map/ppermute | solution.py:14
  117.8 5.2 %collective-permute-start.3 = (f32[16384]{0:T(1024)S(1)}, f32[16384]{0:T(1024)S(1)}, u32[]{:S(2)}, u32[]{:S(2)}) collective-permute-start(f32[16384]{0:T(1024)S(1)} %all_gather.3), channel_id=1, source_target_pairs={{8,0},{16,8},{24,16},{0,24},{9,1},{17,9},{25,17},{1,25},{10,2},{18... | collective-permute-start | bytes 196616 | tf_op jit(solution)/shard_map/ppermute | solution.py:14
Sparse Core Ops, SparseCore 0:
  47.3 54.3 all-reduce.2
where the time goes:
time: 154 us
  waiting for transfers between devices  59.9 us (39%)
  other arithmetic  26 us (17%)
  local copies, waits for them, and re-layouts  24.4 us (16%)
  between operations  14.9 us (10%)
  blocking collectives  14 us (9%)
  matrix products  7.59 us (5%)
  starting transfers between devices  6.97 us (5%)
    unnamed x2, waiting for transfers between devices  53.2 us
    gather x2, local copies, waits for them, and re-layouts, local(): rate = nearby[relative]  23 us
    scatter-add x1, other arithmetic, local(): jax.ops.segment_sum(flat_llr, relative.reshape(-1), num_segments=3 * regi...  21.9 us
    all_gather x1, blocking collectives, local(): own_post = lax.all_gather(owned, 'cluster', axis=0, tiled=True)  14 us
    ppermute x4, starting transfers between devices, passed_along(): return lax.ppermute(block, axis, route)  6.94 us
    ppermute x4, waiting for transfers between devices, passed_along(): return lax.ppermute(block, axis, route)  6.68 us
    dot_general x1, matrix products, local(): jnp.einsum('amr,arl->aml', masked, pilots, preferred_element_type=jnp.flo...  5.3 us
  transfers between devices with their start and end apart: 5, of which 5 were waited for; matrix products, arithmetic and copies ran while one was open for 1% of the time, Pallas kernels for 0%

commit v1 on v0

--- a/solution.py
+++ b/solution.py
@@ -53,7 +53,21 @@
     region_sum = window[region_users : 2 * region_users] + from_below + from_above
     owned_sum = lax.psum_scatter(region_sum, "cluster", scatter_dimension=0, tiled=True)
     owned = decide(owned_sum, own_start, U_DEV, user_cluster, cluster_prior)
-    own_post = lax.all_gather(owned, "cluster", axis=0, tiled=True)
+    ways, here, step = (lax.axis_size("cluster"), lax.axis_index("cluster"), owned.shape[0])
+    dims = [n * ways if d == 0 else n for d, n in enumerate(owned.shape)]
+    full = lax.dynamic_update_slice_in_dim(jnp.zeros(dims, owned.dtype), owned, here * step, axis=0)
+    going_up = going_down = owned
+    for far in range(1, ways // 2 + 1):
+        going_up = lax.ppermute(going_up, "cluster", [(d, (d + 1) % ways) for d in range(ways)])
+        full = lax.dynamic_update_slice_in_dim(full, going_up, (here - far) % ways * step, axis=0)
+        if 2 * far < ways:
+            going_down = lax.ppermute(
+                going_down, "cluster", [(d, (d - 1) % ways) for d in range(ways)]
+            )
+            full = lax.dynamic_update_slice_in_dim(
+                full, going_down, (here + far) % ways * step, axis=0
+            )
+    own_post = full
     below = passed_along(own_post, "region", 1)
     above = passed_along(own_post, "region", -1)
     nearby = jnp.concatenate([below, own_post, above])

time: 154 us -> 161 us (1.045)
  blocking collectives: 14 us -> 0 us
  starting transfers between devices: 6.97 us -> 17.1 us
  waiting for transfers between devices: 59.9 us -> 68.5 us
  local copies, waits for them, and re-layouts: 24.4 us -> 26.3 us
    all_gather x1 -> x0, blocking collectives: 14 us -> none  [local(): own_post = lax.all_gather(owned, 'cluster', axis=0, tiled=True)]
    ppermute x0 -> x7, starting transfers between devices: none -> 10.6 us  [the longest x3 10.6 us: local(): lax.ppermute(going_down, 'cluster', [(d, (d - 1) % ways) for d in range(w...]
    ppermute x0 -> x7, waiting for transfers between devices: none -> 7.15 us  [the longest x4 7.08 us: local(): lax.ppermute(going_up, 'cluster', [(d, (d + 1) % ways) for d in range(way...]
    dynamic_update_slice x0 -> x7, local copies, waits for them, and re-layouts: none -> 1.95 us  [the longest x4 1.03 us: local(): lax.dynamic_update_slice_in_dim(full, going_up, (here - far) % ways * ste...]
  transfers between devices with their start and end apart: 5 -> 12, of which waited for: 5 -> 9; matrix products, arithmetic and copies ran while one was open for 1% -> 2% of each run, Pallas kernels for 0% -> 0%
where the time goes in v1:
time: 161 us; the launch traced here: 160 us
  waiting for transfers between devices  68.5 us (43%)
  local copies, waits for them, and re-layouts  26.3 us (16%)
  other arithmetic  26 us (16%)
  starting transfers between devices  17.1 us (11%)
  between operations  14.9 us (9%)
  matrix products  7.59 us (5%)
    unnamed x2, waiting for transfers between devices  53.2 us
    gather x2, local copies, waits for them, and re-layouts, local(): rate = nearby[relative]  23 us
    scatter-add x1, other arithmetic, local(): jax.ops.segment_sum(flat_llr, relative.reshape(-1), num_segments=3 * regi...  21.9 us
    ppermute x3, starting transfers between devices, local(): lax.ppermute(going_down, 'cluster', [(d, (d - 1) % ways) for d in range(w...  10.6 us
    ppermute x4, waiting for transfers between devices, passed_along(): return lax.ppermute(block, axis, route)  8.14 us
    ppermute x4, waiting for transfers between devices, local(): lax.ppermute(going_up, 'cluster', [(d, (d + 1) % ways) for d in range(way...  7.08 us
    ppermute x4, starting transfers between devices, passed_along(): return lax.ppermute(block, axis, route)  6.43 us
    dot_general x1, matrix products, local(): jnp.einsum('amr,arl->aml', masked, pilots, preferred_element_type=jnp.flo...  5.3 us
  transfers between devices with their start and end apart: 12, of which 9 were waited for; matrix products, arithmetic and copies ran while one was open for 2% of the time, Pallas kernels for 0%

profile of v1, /device:TPU:0, one launch (start us, length us, event | category | flops | bytes accessed | tf_op | source)
XLA Modules:
  0.0 160.4 jit_solution(2412965320872709146)
XLA Ops:
  7.2 0.0 copy-start.2
  7.2 0.0 all-reduce.3.cloned.1.call-start
  7.3 0.0 copy-start
  7.3 0.9 fusion.7
  8.2 0.9 broadcast_compare_fusion
  9.1 0.0 copy-start.4
  9.1 0.0 copy-start.5
  9.1 0.0 copy-start.6
  9.1 5.3 %multiply_reduce_fusion.1 = (f32[4]{0:T(128)S(1)}, f32[4,8,1024]{2,1,0:T(8,128)S(1)}) fusion(f32[4,8,1024]{2,1,0:T(8,128)} %param.14, f32[4]{0:T(128)} %param.15, f32[4,8,1024]{2,1,0:T(8,128)} %param.13, bf16[4,1024,1024]{2,1,0:T(8,128)(2,1)} %param.9, bf16[4,8,1024]{2,1,0:T(8,128)(2,1)} %param.10, pred[4,1024]{1,0:T(4,128)(4,1)S(1)} %broadcast_compare_fusion), kind=kOutput, calls=%fused_computation.10 | convolution fusion | flops 67305472 | bytes 8851488 | tf_op jit(solution)/shard_map/amr,arl->aml/dot_general | solution.py:34
  14.4 0.0 copy-start.1
  14.4 0.0 copy-done.2
  14.4 0.0 copy-done
  14.4 2.3 %multiply_reduce_fusion = (f32[4,1024]{1,0:T(4,128)S(1)}, f32[4,8,1024]{2,1,0:T(8,128)S(1)}) fusion(bf16[4,1024,1024]{2,1,0:T(8,128)(2,1)S(1)} %copy-done, f32[4,8,1024]{2,1,0:T(8,128)S(1)} %get-tuple-element.13, bf16[4,8,1024]{2,1,0:T(8,128)(2,1)S(1)} %copy-done.2, pred[4,1024]{1,0:T(4,128)(4,1)S(1)} %broadcast_compare_fusion), kind=kOutput, calls=%fused_computation.9 | convolution fusion | flops 67301376 | bytes 8736768 | tf_op jit(solution)/shard_map/aml,arl->amr/dot_general | solution.py:38
  16.7 0.0 copy-done.4
  16.7 0.1 select_bitcast_fusion
  16.8 21.9 %scatter_custom_fusion = f32[49152]{0:T(1024)S(1)} fusion(s32[4096]{0:T(1024)S(1)} %bitcast.17, f32[4096]{0:T(1024)S(1)} %bitcast.18, f32[]{:T(128)} %constant.105.clone.1), kind=kCustom, calls=%fused_computation.11 | custom fusion | flops 4096 | bytes 196612 | tf_op jit(solution)/shard_map/scatter-add | solution.py:50
  38.8 3.0 %collective-permute-start = (f32[16384]{0:T(1024)S(1)}, f32[16384]{0:T(1024)S(1)}, u32[]{:S(2)}, u32[]{:S(2)}) collective-permute-start(f32[16384]{0:T(1024)S(1)} %get-tuple-element.5), channel_id=1, source_target_pairs={{24,0},{0,8},{8,16},{16,24},{25,1},{1,9},{9,17},{17,25},{26,2},{2,... | collective-permute-start | bytes 196616 | tf_op jit(solution)/shard_map/ppermute | solution.py:14
  41.8 1.0 collective-permute-start.1
  42.8 0.7 dynamic_slice.3
  43.5 1.6 %collective-permute-done = f32[16384]{0:T(1024)S(1)} collective-permute-done((f32[16384]{0:T(1024)S(1)}, f32[16384]{0:T(1024)S(1)}, u32[]{:S(2)}, u32[]{:S(2)}) %collective-permute-start) | collective-permute-done | bytes 65568 | tf_op jit(solution)/shard_map/ppermute | solution.py:14
  45.1 1.4 collective-permute-done.1
  46.5 0.6 fusion.3
  47.1 0.0 all-reduce.3.cloned.1.call-update
  47.2 0.0 copy-done.5
  47.2 0.1 select_reduce_fusion
  47.3 0.0 copy-done.6
  47.3 0.6 dynamic-slice
  48.5 53.2 %all-reduce.3.cloned.1.call-done = f32[16384]{0:T(1024)} async-done(((f32[16384]{0:T(1024)}), f32[16384]{0:T(1024)}) %all-reduce.3.cloned.1.call-update) | async-done | bytes 65552
  101.7 0.7 fusion.17
  102.4 0.0 copy-start.3
  102.4 0.1 collective-permute-start.2
  102.5 3.5 %collective-permute-start.3 = (f32[2048]{0:T(1024)S(1)}, f32[2048]{0:T(1024)S(1)}, u32[]{:S(2)}, u32[]{:S(2)}) collective-permute-start(f32[2048]{0:T(1024)S(1)} %get-tuple-element.4), channel_id=1, source_target_pairs={{0,7},{1,0},{2,1},{3,2},{4,3},{5,4},{6,5},{7,6},{8,15},{9,8},{10,9... | collective-permute-start | bytes 24584 | tf_op jit(solution)/shard_map/ppermute | solution.py:64
  106.0 1.3 collective-permute-done.2
  107.3 0.0 collective-permute-start.4
  107.3 0.0 collective-permute-done.3
  107.4 3.5 %collective-permute-start.5 = (f32[2048]{0:T(1024)S(1)}, f32[2048]{0:T(1024)S(1)}, u32[]{:S(2)}, u32[]{:S(2)}) collective-permute-start(f32[2048]{0:T(1024)S(1)} %collective-permute-done.3), channel_id=1, source_target_pairs={{0,7},{1,0},{2,1},{3,2},{4,3},{5,4},{6,5},{7,6},{8,15},{9,8},{10,9... | collective-permute-start | bytes 24584 | tf_op jit(solution)/shard_map/ppermute | solution.py:64
  110.9 1.3 collective-permute-done.4
  112.2 0.0 collective-permute-start.6
  112.2 0.0 collective-permute-done.5
  112.2 3.5 %collective-permute-start.7 = (f32[2048]{0:T(1024)S(1)}, f32[2048]{0:T(1024)S(1)}, u32[]{:S(2)}, u32[]{:S(2)}) collective-permute-start(f32[2048]{0:T(1024)S(1)} %collective-permute-done.5), channel_id=1, source_target_pairs={{0,7},{1,0},{2,1},{3,2},{4,3},{5,4},{6,5},{7,6},{8,15},{9,8},{10,9... | collective-permute-start | bytes 24584 | tf_op jit(solution)/shard_map/ppermute | solution.py:64
  115.8 1.3 collective-permute-done.6
  117.1 0.0 collective-permute-start.8
  117.1 0.2 dynamic_update_slice.25
  117.3 0.3 dynamic_update_slice.26
  117.6 0.3 dynamic_update_slice.27
  117.9 0.3 dynamic_update_slice.28
  118.2 0.3 dynamic_update_slice.29
  118.5 0.0 collective-permute-done.7
  118.5 0.3 dynamic_update_slice.30
  118.9 3.1 %collective-permute-done.8 = f32[2048]{0:T(1024)S(1)} collective-permute-done((f32[2048]{0:T(1024)S(1)}, f32[2048]{0:T(1024)S(1)}, u32[]{:S(2)}, u32[]{:S(2)}) %collective-permute-start.8) | collective-permute-done | bytes 8224 | tf_op jit(solution)/shard_map/ppermute | solution.py:61
  122.0 0.2 dynamic_update_slice.31
  122.1 2.4 %collective-permute-start.10 = (f32[16384]{0:T(1024)S(1)}, f32[16384]{0:T(1024)S(1)}, u32[]{:S(2)}, u32[]{:S(2)}) collective-permute-start(f32[16384]{0:T(1024)S(1)} %dynamic_update_slice.31), channel_id=1, source_target_pairs={{8,0},{16,8},{24,16},{0,24},{9,1},{17,9},{25,17},{1,25},{10,2},{18... | collective-permute-start | bytes 196616 | tf_op jit(solution)/shard_map/ppermute | solution.py:14
  124.6 0.0 collective-permute-start.9
  124.6 1.9 %collective-permute-done.10 = f32[16384]{0:T(1024)S(1)} collective-permute-done((f32[16384]{0:T(1024)S(1)}, f32[16384]{0:T(1024)S(1)}, u32[]{:S(2)}, u32[]{:S(2)}) %collective-permute-start.10) | collective-permute-done | bytes 65568 | tf_op jit(solution)/shard_map/ppermute | solution.py:14
  126.5 3.3 %collective-permute-done.9 = f32[16384]{0:T(1024)S(1)} collective-permute-done((f32[16384]{0:T(1024)S(1)}, f32[16384]{0:T(1024)S(1)}, u32[]{:S(2)}, u32[]{:S(2)}) %collective-permute-start.9) | collective-permute-done | bytes 65568 | tf_op jit(solution)/shard_map/ppermute | solution.py:14
  129.7 23.0 %gather_fusion = f32[4096]{0:T(1024)S(1)} fusion(f32[49152]{0:T(1024)S(1)} %pad_maximum_fusion, s32[4096]{0:T(1024)S(1)} %bitcast_clamp_fusion), kind=kCustom, calls=%fused_computation | custom fusion | bytes 49152 | tf_op jit(solution)/shard_map/gather | solution.py:74
  152.8 0.0 copy-done.1
  152.8 0.0 copy-done.3
  152.8 0.7 select_convert_fusion
  (9 shorter events, 0.1 us)
Async XLA Ops:
  7.2 7.2 %copy-start.2 = (bf16[4,8,1024]{2,1,0:T(8,128)(2,1)S(1)}, bf16[4,8,1024]{2,1,0:T(8,128)(2,1)}, u32[]{:S(2)}) copy-start(bf16[4,8,1024]{2,1,0:T(8,128)(2,1)} %param.10) | copy-start | bytes 196612
  7.2 94.5 %all-reduce.3.cloned.1.call-start = ((), (), s32[]{:S(2)}) async-start(), calls=%async_computation | async-start | bytes 131072
  7.3 7.1 %copy-start = (bf16[4,1024,1024]{2,1,0:T(8,128)(2,1)S(1)}, bf16[4,1024,1024]{2,1,0:T(8,128)(2,1)}, u32[]{:S(2)}) copy-start(bf16[4,1024,1024]{2,1,0:T(8,128)(2,1)} %param.9) | copy-start | bytes 25165828
  9.1 7.7 %copy-start.4 = (s32[4]{0:T(128)S(1)}, s32[4]{0:T(128)}, u32[]{:S(2)}) copy-start(s32[4]{0:T(128)} %param.12) | copy-start | bytes 52
  9.1 38.1 %copy-start.5 = (f32[16]{0:T(128)S(1)}, f32[16]{0:T(128)}, u32[]{:S(2)}) copy-start(f32[16]{0:T(128)} %param.17) | copy-start | bytes 196
  9.1 38.2 %copy-start.6 = (u32[32]{0:T(128)S(1)}, u32[32]{0:T(128)}, u32[]{:S(2)}) copy-start(u32[32]{0:T(128)} %constant.136) | copy-start | bytes 388
  14.4 138.4 %copy-start.1 = (f32[4,8,1024]{2,1,0:T(8,128)}, f32[4,8,1024]{2,1,0:T(8,128)S(1)}, u32[]{:S(2)}) copy-start(f32[4,8,1024]{2,1,0:T(8,128)S(1)} %get-tuple-element.13) | copy-start | bytes 393220
  38.8 6.3 %collective-permute-start = (f32[16384]{0:T(1024)S(1)}, f32[16384]{0:T(1024)S(1)}, u32[]{:S(2)}, u32[]{:S(2)}) collective-permute-start(f32[16384]{0:T(1024)S(1)} %get-tuple-element.5), channel_id=1, source_target_pairs={{24,0},{0,8},{8,16},{16,24},{25,1},{1,9},{9,17},{17,25},{26,2},{2,... | collective-permute-start | bytes 196616 | tf_op jit(solution)/shard_map/ppermute | solution.py:14
  41.8 4.7 %collective-permute-start.1 = (f32[16384]{0:T(1024)S(1)}, f32[16384]{0:T(1024)S(1)}, u32[]{:S(2)}, u32[]{:S(2)}) collective-permute-start(f32[16384]{0:T(1024)S(1)} %get-tuple-element.6), channel_id=1, source_target_pairs={{8,0},{16,8},{24,16},{0,24},{9,1},{17,9},{25,17},{1,25},{10,2},{18... | collective-permute-start | bytes 196616 | tf_op jit(solution)/shard_map/ppermute | solution.py:14
  102.4 50.4 %copy-start.3 = (f32[2048]{0:T(1024)}, f32[2048]{0:T(1024)S(1)}, u32[]{:S(2)}) copy-start(f32[2048]{0:T(1024)S(1)} %get-tuple-element.4) | copy-start | bytes 24580
  102.4 4.9 %collective-permute-start.2 = (f32[2048]{0:T(1024)S(1)}, f32[2048]{0:T(1024)S(1)}, u32[]{:S(2)}, u32[]{:S(2)}) collective-permute-start(f32[2048]{0:T(1024)S(1)} %get-tuple-element.4), channel_id=1, source_target_pairs={{0,1},{1,2},{2,3},{3,4},{4,5},{5,6},{6,7},{7,0},{8,9},{9,10},{10,1... | collective-permute-start | bytes 24584 | tf_op jit(solution)/shard_map/ppermute | solution.py:61
  102.5 4.9 %collective-permute-start.3 = (f32[2048]{0:T(1024)S(1)}, f32[2048]{0:T(1024)S(1)}, u32[]{:S(2)}, u32[]{:S(2)}) collective-permute-start(f32[2048]{0:T(1024)S(1)} %get-tuple-element.4), channel_id=1, source_target_pairs={{0,7},{1,0},{2,1},{3,2},{4,3},{5,4},{6,5},{7,6},{8,15},{9,8},{10,9... | collective-permute-start | bytes 24584 | tf_op jit(solution)/shard_map/ppermute | solution.py:64
  107.3 4.9 %collective-permute-start.4 = (f32[2048]{0:T(1024)S(1)}, f32[2048]{0:T(1024)S(1)}, u32[]{:S(2)}, u32[]{:S(2)}) collective-permute-start(f32[2048]{0:T(1024)S(1)} %collective-permute-done.2), channel_id=1, source_target_pairs={{0,1},{1,2},{2,3},{3,4},{4,5},{5,6},{6,7},{7,0},{8,9},{9,10},{10,1... | collective-permute-start | bytes 24584 | tf_op jit(solution)/shard_map/ppermute | solution.py:61
  107.4 4.9 %collective-permute-start.5 = (f32[2048]{0:T(1024)S(1)}, f32[2048]{0:T(1024)S(1)}, u32[]{:S(2)}, u32[]{:S(2)}) collective-permute-start(f32[2048]{0:T(1024)S(1)} %collective-permute-done.3), channel_id=1, source_target_pairs={{0,7},{1,0},{2,1},{3,2},{4,3},{5,4},{6,5},{7,6},{8,15},{9,8},{10,9... | collective-permute-start | bytes 24584 | tf_op jit(solution)/shard_map/ppermute | solution.py:64
  112.2 4.9 %collective-permute-start.6 = (f32[2048]{0:T(1024)S(1)}, f32[2048]{0:T(1024)S(1)}, u32[]{:S(2)}, u32[]{:S(2)}) collective-permute-start(f32[2048]{0:T(1024)S(1)} %collective-permute-done.4), channel_id=1, source_target_pairs={{0,1},{1,2},{2,3},{3,4},{4,5},{5,6},{6,7},{7,0},{8,9},{9,10},{10,1... | collective-permute-start | bytes 24584 | tf_op jit(solution)/shard_map/ppermute | solution.py:61
  112.2 6.3 %collective-permute-start.7 = (f32[2048]{0:T(1024)S(1)}, f32[2048]{0:T(1024)S(1)}, u32[]{:S(2)}, u32[]{:S(2)}) collective-permute-start(f32[2048]{0:T(1024)S(1)} %collective-permute-done.5), channel_id=1, source_target_pairs={{0,7},{1,0},{2,1},{3,2},{4,3},{5,4},{6,5},{7,6},{8,15},{9,8},{10,9... | collective-permute-start | bytes 24584 | tf_op jit(solution)/shard_map/ppermute | solution.py:64
  117.1 4.9 %collective-permute-start.8 = (f32[2048]{0:T(1024)S(1)}, f32[2048]{0:T(1024)S(1)}, u32[]{:S(2)}, u32[]{:S(2)}) collective-permute-start(f32[2048]{0:T(1024)S(1)} %collective-permute-done.6), channel_id=1, source_target_pairs={{0,1},{1,2},{2,3},{3,4},{4,5},{5,6},{6,7},{7,0},{8,9},{9,10},{10,1... | collective-permute-start | bytes 24584 | tf_op jit(solution)/shard_map/ppermute | solution.py:61
  122.1 4.3 %collective-permute-start.10 = (f32[16384]{0:T(1024)S(1)}, f32[16384]{0:T(1024)S(1)}, u32[]{:S(2)}, u32[]{:S(2)}) collective-permute-start(f32[16384]{0:T(1024)S(1)} %dynamic_update_slice.31), channel_id=1, source_target_pairs={{8,0},{16,8},{24,16},{0,24},{9,1},{17,9},{25,17},{1,25},{10,2},{18... | collective-permute-start | bytes 196616 | tf_op jit(solution)/shard_map/ppermute | solution.py:14
  124.6 5.2 %collective-permute-start.9 = (f32[16384]{0:T(1024)S(1)}, f32[16384]{0:T(1024)S(1)}, u32[]{:S(2)}, u32[]{:S(2)}) collective-permute-start(f32[16384]{0:T(1024)S(1)} %dynamic_update_slice.31), channel_id=1, source_target_pairs={{24,0},{0,8},{8,16},{16,24},{25,1},{1,9},{9,17},{17,25},{26,2},{2,... | collective-permute-start | bytes 196616 | tf_op jit(solution)/shard_map/ppermute | solution.py:14
Sparse Core Ops, SparseCore 0:
  47.3 54.3 all-reduce.2
